TPU v7x, 32 devices: a whole 2x2x4 slice. The times are simulated.
32 devices in a mesh: rep: 2 (over y), step: 4 (over z), patch: 4 (over x, core).
Axes of the slice: x: 2, y: 2, z: 4, core: 2. Of those that a mesh axis runs over, the one named last changes fastest.
Arguments:
- latent_old: float32 [8, 1024, 64], P(('rep', 'step'), 'patch'), parts along dimension 0, may hold values from -6 to 6
- noise_start: float32 [2048, 64], P(('rep', 'patch')), parts along dimension 0, may hold values from -6 to 6
- step_index: int32 [8], P(('rep', 'step')), parts along dimension 0, may hold values from 0 to 998
- sigma_table: float32 [1000], replicated, may hold values from 0.02 to 1
- mod_weight: bfloat16 [256, 9216], replicated, may hold values from -0.375 to 0.375
- embed_weight: bfloat16 [64, 3072], replicated, may hold values from -0.75 to 0.75
- embed_bias: float32 [3072], replicated, may hold values from -3 to 3
- query_weight: bfloat16 [3072, 1536], P('step'), may hold values from -0.109375 to 0.109375
- query_gain: float32 [128], replicated, may hold values from 0.1 to 1.9
- stale_keys: bfloat16 [8, 1280, 1536], P(('rep', 'step'), 'patch'), parts along dimension 0, may hold values from -640 to 640
- stale_values: bfloat16 [8, 1280, 1536], P(('rep', 'step'), 'patch'), parts along dimension 0, may hold values from -6 to 6
- out_weight: bfloat16 [3072, 1536], P('step'), may hold values from -0.3125 to 0.3125
- final_weight: bfloat16 [3072, 64], replicated, may hold values from -0.109375 to 0.109375
Outputs:
- latent_new: float32 [8, 1024, 64], P(('rep', 'step'), 'patch'), parts along dimension 0
There are 2 independent parts, one for each index of `rep`. A program takes and returns all parts, laid end to end along the dimension named above; an argument that names none is the same for every part. Nothing has to cross between parts.
All inputs are finite; a program needn't handle non-finite values.
Results may differ from a plain program's by a relative error of at most 0.012.
The roundings to bfloat16 on the way count: a program that leaves them out, or rounds other values in their place, can miss the bound.
Values may be sent and summed in bfloat16 or wider, within the bound.
A program may use at most 128 MiB of HBM per device.

v0:
```python
import math

import jax
import jax.numpy as jnp
from jax import lax
from jax.sharding import PartitionSpec as P

D = 3072
HEAD = 128
FREQ = 256
HEADS = 12


epsilon = 1e-06


def entering(shard, axis, join, neutral):
    place = lax.axis_index(axis)
    gathered = lax.all_gather(shard.astype(jnp.bfloat16), axis)
    state = jnp.zeros_like(shard) + jnp.asarray(neutral, shard.dtype)

    def one(hop, state):
        return join(state, lax.dynamic_index_in_dim(gathered, hop, 0, False).astype(shard.dtype))

    return lax.fori_loop(0, place, one, state)


def layer_norm(values_in):
    row_mean = jnp.mean(values_in, axis=-1, keepdims=True)
    centered = values_in - row_mean
    row_var = jnp.mean(centered * centered, axis=-1, keepdims=True)
    return centered * lax.rsqrt(row_var + epsilon)


def time_embed(sigma_now):
    half_count = FREQ // 2
    frequency = jnp.exp(
        -math.log(10000.0) * jnp.arange(half_count).astype(jnp.float32) / half_count
    )
    angles = 1000.0 * sigma_now * frequency
    return jnp.concatenate([jnp.cos(angles), jnp.sin(angles)])


def project_back(attended, weight_rows):
    return lax.dot_general(
        attended, weight_rows, (((1,), (1,)), ((), ())), preferred_element_type=jnp.float32
    )


def norm_queries(raw_queries, query_gain):
    token_count = raw_queries.shape[0]
    head_count = raw_queries.shape[1] // HEAD
    queries = raw_queries.reshape(token_count, head_count, HEAD)
    queries = (
        queries
        * lax.rsqrt(jnp.mean(queries * queries, axis=-1, keepdims=True) + epsilon)
        * query_gain
    )
    return queries.astype(jnp.bfloat16)


def empty_state(queries):
    token_count = queries.shape[0]
    head_count = queries.shape[1]
    return (
        jnp.full((head_count, token_count), -jnp.inf, jnp.float32),
        jnp.zeros((head_count, token_count), jnp.float32),
        jnp.zeros((head_count, token_count, HEAD), jnp.float32),
    )


def attend_block(queries, state_tuple, key_piece, value_piece):
    head_count = queries.shape[1]
    row_count = key_piece.shape[0]
    key_split = key_piece.reshape(row_count, head_count, HEAD)
    value_split = value_piece.reshape(row_count, head_count, HEAD)
    run_peak, run_total, run_sum = state_tuple
    scores = jnp.einsum(
        "qhd,khd->hqk", queries, key_split, preferred_element_type=jnp.float32
    ) / math.sqrt(HEAD)
    new_peak = jnp.max(scores, axis=-1)
    rescale = jnp.exp(run_peak - new_peak)
    exp_weights = jnp.exp(scores - new_peak[..., None])
    run_total = run_total * rescale + jnp.sum(exp_weights, axis=-1)
    run_sum = run_sum * rescale[..., None] + jnp.einsum(
        "hqk,khd->hqd",
        exp_weights.astype(jnp.bfloat16),
        value_split,
        preferred_element_type=jnp.float32,
    )
    return (new_peak, run_total, run_sum)


def finish_heads(state_tuple):
    final_peak, final_total, final_sum = state_tuple
    blended = final_sum / final_total[..., None]
    token_count = blended.shape[1]
    return jnp.transpose(blended, (1, 0, 2)).reshape(token_count, -1).astype(jnp.bfloat16)


def per_device(
    latent_old,
    noise_start,
    step_index,
    sigma_table,
    mod_weight,
    embed_weight,
    embed_bias,
    query_weight,
    query_gain,
    stale_keys,
    stale_values,
    out_weight,
    final_weight,
):
    step_slot = step_index[0]
    table_slots = jnp.arange(sigma_table.shape[0])
    sigma_now = jnp.sum(jnp.where(table_slots == step_slot, sigma_table, 0.0))
    sigma_next = jnp.sum(jnp.where(table_slots == step_slot + 1, sigma_table, 0.0))
    embedded = jax.nn.silu(time_embed(sigma_now)).astype(jnp.bfloat16)
    modulate = jnp.dot(embedded[None, :], mod_weight, preferred_element_type=jnp.float32)[0]
    width = D
    shift_vec = modulate[:width]
    scale_vec = modulate[width : 2 * width]
    gate_vec = modulate[2 * width :]
    latent = latent_old[0]
    token_count = latent.shape[0]
    hidden = (
        jnp.dot(latent.astype(jnp.bfloat16), embed_weight, preferred_element_type=jnp.float32)
        + embed_bias
    )
    normed = (layer_norm(hidden) * (1.0 + scale_vec) + shift_vec).astype(jnp.bfloat16)
    patch_count = lax.axis_size("patch")
    group_width = HEADS // patch_count * HEAD
    patch_slot = lax.axis_index("patch")
    query_columns = lax.dynamic_slice_in_dim(query_weight, patch_slot * group_width, group_width, 1)
    normed_every = lax.all_gather(normed, "patch", axis=0, tiled=True)
    raw_every = jnp.dot(
        normed_every,
        lax.all_gather(query_columns, "step", axis=0, tiled=True),
        preferred_element_type=jnp.float32,
    )
    queries_every = norm_queries(raw_every, query_gain)
    keys_group, values_group = (
        lax.all_to_all(stale_keys[0], "patch", split_axis=1, concat_axis=0, tiled=True),
        lax.all_to_all(stale_values[0], "patch", split_axis=1, concat_axis=0, tiled=True),
    )
    state_every = attend_block(queries_every, empty_state(queries_every), keys_group, values_group)
    attended_every = finish_heads(state_every)
    attended = lax.all_to_all(attended_every, "patch", split_axis=0, concat_axis=1, tiled=True)
    branch = project_back(attended, lax.all_gather(out_weight, "step", axis=0, tiled=True))
    mixed = hidden + gate_vec * branch
    velocity = jnp.dot(
        layer_norm(mixed).astype(jnp.bfloat16), final_weight, preferred_element_type=jnp.float32
    )
    drift_term = velocity * (sigma_next - sigma_now)
    flat_term = drift_term.reshape(-1, 128)

    def add_terms(earlier, later):
        return earlier + later

    prefix = entering(flat_term, "step", add_terms, jnp.zeros_like(flat_term))
    result = noise_start + (prefix + flat_term).reshape(token_count, -1)
    return result[None]


def solution(mesh):
    placed = (
        P(("rep", "step"), "patch", None),
        P(("rep", "patch"), None),
        P(("rep", "step")),
        P(),
        P(),
        P(),
        P(),
        P("step", None),
        P(),
        P(("rep", "step"), "patch", None),
        P(("rep", "step"), "patch", None),
        P("step", None),
        P(),
    )
    return jax.shard_map(
        per_device,
        mesh=mesh,
        in_specs=placed,
        out_specs=P(("rep", "step"), "patch", None),
        check_vma=False,
    )
```

profile of v0, /device:TPU:0, one launch (start us, length us, event | category | flops | bytes accessed | tf_op | source)
XLA Modules:
  0.0 305.8 jit_solution(14107807590935253234)
XLA Ops:
  17.8 2.7 all_to_all.36
  20.5 2.3 copy.38
  22.8 4.2 %all-to-all-start = ((bf16[320,4,384]{2,0,1:T(8,128)(2,1)}), bf16[320,4,384]{2,0,1:T(8,128)(2,1)}, u32[]{:S(2)}, u32[]{:S(2)}) async-start(bf16[320,4,384]{2,0,1:T(8,128)(2,1)} %copy.38), calls=%async_computation | async-start | bytes 1966080 | tf_op jit(solution)/shard_map/all_to_all | solution.py:145
  27.0 2.7 all_to_all.39
  29.7 2.3 copy.41
  32.0 9.4 %all-to-all-done = bf16[320,4,384]{2,0,1:T(8,128)(2,1)} async-done(((bf16[320,4,384]{2,0,1:T(8,128)(2,1)}), bf16[320,4,384]{2,0,1:T(8,128)(2,1)}, u32[]{:S(2)}, u32[]{:S(2)}) %all-to-all-start) | async-done | bytes 983072 | tf_op jit(solution)/shard_map/all_to_all | solution.py:145
  41.5 4.4 %all-to-all-start.1 = ((bf16[320,4,384]{2,0,1:T(8,128)(2,1)}), bf16[320,4,384]{2,0,1:T(8,128)(2,1)}, u32[]{:S(2)}, u32[]{:S(2)}) async-start(bf16[320,4,384]{2,0,1:T(8,128)(2,1)} %copy.41), calls=%async_computation.1 | async-start | bytes 1966080 | tf_op jit(solution)/shard_map/all_to_all | solution.py:146
  45.9 3.7 %reshape.109 = bf16[1280,3,128]{2,1,0:T(4,128)(2,1)} reshape(bf16[4,320,384]{2,1,0:T(8,128)(2,1)} %bitcast.5) | data formatting | bytes 1966080 | tf_op jit(solution)/shard_map/reshape | solution.py:75
  49.6 9.9 %all-to-all-done.1 = bf16[320,4,384]{2,0,1:T(8,128)(2,1)} async-done(((bf16[320,4,384]{2,0,1:T(8,128)(2,1)}), bf16[320,4,384]{2,0,1:T(8,128)(2,1)}, u32[]{:S(2)}, u32[]{:S(2)}) %all-to-all-start.1) | async-done | bytes 983072 | tf_op jit(solution)/shard_map/all_to_all | solution.py:146
  59.5 3.7 %reshape.110 = bf16[1280,3,128]{2,1,0:T(4,128)(2,1)} reshape(bf16[4,320,384]{2,1,0:T(8,128)(2,1)} %bitcast.7) | data formatting | bytes 1966080 | tf_op jit(solution)/shard_map/reshape | solution.py:76
  63.2 45.6 %all-gather.4.cloned.1.call-done = bf16[1024,3072]{1,0:T(8,128)(2,1)} async-done(((bf16[256,3072]{1,0:T(8,128)(2,1)}), bf16[1024,3072]{1,0:T(8,128)(2,1)}) %all-gather.4.cloned.1.call-update) | async-done | bytes 6291472 | tf_op jit(solution)/shard_map/all_gather | solution.py:137
  108.7 7.3 %fusion.31 = f32[1024,384]{0,1:T(8,128)} fusion(bf16[1024,3072]{1,0:T(8,128)(2,1)} %all-gather.4.cloned.1.call-done, bf16[3072,384]{1,0:T(8,128)(2,1)} %all-gather.6.cloned.1.call-done), kind=kOutput, calls=%fused_computation.57 | convolution fusion | flops 2415919104 | bytes 10223616 | tf_op jit(solution)/shard_map/dot_general | solution.py:138
  116.0 3.3 %copy.37 = f32[1024,3,128]{2,0,1:T(8,128)} copy(f32[1024,3,128]{0,2,1:T(8,128)} %bitcast.44) | data formatting | bytes 3145728 | tf_op jit(solution)/shard_map/reshape | solution.py:53
  121.1 4.4 %multiply_reduce_fusion = (f32[3,1024]{1,0:T(4,128)S(1)}, f32[3,1024,1280]{2,1,0:T(8,128)S(1)}) fusion(bf16[1280,3,128]{2,1,0:T(4,128)(2,1)} %reshape.109, f32[1024,3,128]{2,0,1:T(8,128)} %copy.37, f32[128]{0:T(128)S(1)} %copy-done.6, f32[1024,3]{0,1:T(4,128)S(1)} %add_rsqrt_fusion), kind=kOutput, calls=%fused_computation.2 | convolution fusion | flops 1015673856 | bytes 18309632 | tf_op jit(solution)/shard_map/qhd,khd->hqk/dot_general | solution.py:78
  125.6 3.3 %fusion = f32[3,1024]{1,0:T(4,128)S(1)} fusion(f32[3,1024,1280]{2,1,0:T(8,128)S(1)} %get-tuple-element.45, f32[3,1024]{1,0:T(4,128)S(1)} %get-tuple-element.44), kind=kLoop, calls=%fused_computation.3 | loop fusion | flops 11793408 | bytes 15753216 | tf_op jit(solution)/shard_map/reduce_sum | solution.py:84
  128.9 4.5 %fusion.9 = bf16[1024,3,128]{2,0,1:T(8,128)(2,1)} fusion(f32[3,1024,1280]{2,1,0:T(8,128)S(1)} %get-tuple-element.45, f32[3,1024]{1,0:T(4,128)S(1)} %get-tuple-element.44, bf16[1280,3,128]{2,1,0:T(4,128)(2,1)S(1)} %copy-done.3, f32[1024,3]{0,1:T(4,128)S(1)} %bitcast_add_fusion.1, f32[1024,3]{0,1:T(4,128)S(1)} %multiply_bitcast_fusion), kind=kOutput, calls=%fused_computation.18 | convolution fusion | flops 1019609088 | bytes 17534976 | tf_op jit(solution)/shard_map/hqk,khd->hqd/dot_general | solution.py:85
  133.4 2.3 copy.44
  135.7 2.6 convert_element_type.59
  138.3 2.1 copy.45
  140.5 4.2 %all-to-all-start.2 = ((bf16[4,256,384]{1,2,0:T(8,128)(2,1)}), bf16[4,256,384]{1,2,0:T(8,128)(2,1)}, u32[]{:S(2)}, u32[]{:S(2)}) async-start(bf16[4,256,384]{1,2,0:T(8,128)(2,1)} %copy.45), calls=%async_computation.2 | async-start | bytes 1572864 | tf_op jit(solution)/shard_map/all_to_all | solution.py:150
  146.1 10.3 %all-to-all-done.2 = bf16[4,256,384]{1,2,0:T(8,128)(2,1)} async-done(((bf16[4,256,384]{1,2,0:T(8,128)(2,1)}), bf16[4,256,384]{1,2,0:T(8,128)(2,1)}, u32[]{:S(2)}, u32[]{:S(2)}) %all-to-all-start.2) | async-done | bytes 786464 | tf_op jit(solution)/shard_map/all_to_all | solution.py:150
  156.4 120.7 %all-gather.8.cloned.1.call-done = bf16[3072,1536]{1,0:T(8,128)(2,1)} async-done(((bf16[768,1536]{1,0:T(8,128)(2,1)}), bf16[3072,1536]{1,0:T(8,128)(2,1)}) %all-gather.8.cloned.1.call-update) | async-done | bytes 9437200 | tf_op jit(solution)/shard_map/all_gather | solution.py:151
  277.1 5.6 %fusion.28 = (f32[256]{0:T(256)S(1)}, f32[256,3072]{1,0:T(8,128)S(1)}) fusion(f32[256,3072]{1,0:T(8,128)S(1)} %get-tuple-element.43, bf16[256,1536]{0,1:T(8,128)(2,1)} %bitcast.11, bf16[3072,1536]{1,0:T(8,128)(2,1)} %all-gather.8.cloned.1.call-done, f32[3072]{0:T(1024)S(1)} %get-tuple-element.39), kind=kOutput, calls=%fused_computation.54 | convolution fusion | flops 2418278144 | bytes 16528384 | tf_op jit(solution)/shard_map/dot_general | solution.py:45
  284.7 13.6 %all_gather.16 = bf16[4,128,128]{2,1,0:T(8,128)(2,1)S(1)} all-gather(bf16[1,128,128]{2,1,0:T(8,128)(2,1)S(1)} %convert_element_type.62), channel_id=1, replica_groups=mesh['rep'=2,'step'=4,'patch'=4] {'step'}, dimensions={0}, use_global_device_ids=true | all-gather | bytes 163840 | tf_op jit(solution)/shard_map/all_gather | solution.py:19
  (52 shorter events, 14.6 us)
Async XLA Ops:
  6.5 1.7 copy-start
  6.5 56.6 %all-gather.6.cloned.1.call-start = ((), (), s32[]{:S(2)}) async-start(), calls=%async_computation.4 | async-start | bytes 2949120 | tf_op jit(solution)/shard_map/all_gather | solution.py:140
  9.1 99.6 %all-gather.4.cloned.1.call-start = ((), (), s32[]{:S(2)}) async-start(), calls=%async_computation.3 | async-start | bytes 7864320 | tf_op jit(solution)/shard_map/all_gather | solution.py:137
  11.9 2.5 copy-start.2
  17.0 260.1 %all-gather.8.cloned.1.call-start = ((), (), s32[]{:S(2)}) async-start(), calls=%async_computation.5 | async-start | bytes 11796480 | tf_op jit(solution)/shard_map/all_gather | solution.py:151
  22.8 18.6 %all-to-all-start = ((bf16[320,4,384]{2,0,1:T(8,128)(2,1)}), bf16[320,4,384]{2,0,1:T(8,128)(2,1)}, u32[]{:S(2)}, u32[]{:S(2)}) async-start(bf16[320,4,384]{2,0,1:T(8,128)(2,1)} %copy.38), calls=%async_computation | async-start | bytes 1966080 | tf_op jit(solution)/shard_map/all_to_all | solution.py:145
  41.5 18.0 %all-to-all-start.1 = ((bf16[320,4,384]{2,0,1:T(8,128)(2,1)}), bf16[320,4,384]{2,0,1:T(8,128)(2,1)}, u32[]{:S(2)}, u32[]{:S(2)}) async-start(bf16[320,4,384]{2,0,1:T(8,128)(2,1)} %copy.41), calls=%async_computation.1 | async-start | bytes 1966080 | tf_op jit(solution)/shard_map/all_to_all | solution.py:146
  116.0 5.1 %copy-start.6 = (f32[128]{0:T(128)S(1)}, f32[128]{0:T(128)}, u32[]{:S(2)}) copy-start(f32[128]{0:T(128)} %param.23) | copy-start | bytes 1540
  125.5 3.4 %copy-start.3 = (bf16[1280,3,128]{2,1,0:T(4,128)(2,1)S(1)}, bf16[1280,3,128]{2,1,0:T(4,128)(2,1)}, u32[]{:S(2)}) copy-start(bf16[1280,3,128]{2,1,0:T(4,128)(2,1)} %reshape.110) | copy-start | bytes 2949124
  133.4 12.5 %copy-start.5 = (f32[256,64]{0,1:T(8,128)S(1)}, f32[256,64]{0,1:T(8,128)}, u32[]{:S(2)}) copy-start(f32[256,64]{0,1:T(8,128)} %param.16) | copy-start | bytes 196612
  140.5 15.9 %all-to-all-start.2 = ((bf16[4,256,384]{1,2,0:T(8,128)(2,1)}), bf16[4,256,384]{1,2,0:T(8,128)(2,1)}, u32[]{:S(2)}, u32[]{:S(2)}) async-start(bf16[4,256,384]{1,2,0:T(8,128)(2,1)} %copy.45), calls=%async_computation.2 | async-start | bytes 1572864 | tf_op jit(solution)/shard_map/all_to_all | solution.py:150
  282.7 1.0 copy-start.4
  283.2 16.1 %copy-start.1 = (bf16[768,1536]{1,0:T(8,128)(2,1)S(1)}, bf16[768,1536]{1,0:T(8,128)(2,1)}, u32[]{:S(2)}) copy-start(bf16[768,1536]{1,0:T(8,128)(2,1)} %param.22) | copy-start | bytes 7077892
Sparse Core Ops, SparseCore 0:
  9.2 52.7 all-gather.5
  63.6 45.1 all-gather.3
  110.3 166.7 all-gather.7
where the time goes:
time: 307 us; the launch traced here: 306 us
  waiting for transfers between devices  197 us (64%)
  local copies, waits for them, and re-layouts  32.3 us (11%)
  matrix products  25 us (8%)
  between operations  15.9 us (5%)
  blocking collectives  13.6 us (4%)
  starting transfers between devices  12.9 us (4%)
  other arithmetic  9.39 us (3%)
    all_gather x1, waiting for transfers between devices, per_device(): lax.all_gather(out_weight, 'step', axis=0, tiled=True)  121 us
    all_gather x1, waiting for transfers between devices, per_device(): normed_every = lax.all_gather(normed, 'patch', axis=0, tiled=True)  45.6 us
    all_gather x1, blocking collectives, entering(): gathered = lax.all_gather(shard.astype(jnp.bfloat16), axis)  13.6 us
    all_to_all x1, waiting for transfers between devices, per_device(): lax.all_to_all(attended_every, 'patch', split_axis=0, concat_axis=1, tile...  10.3 us
    all_to_all x1, waiting for transfers between devices, per_device(): lax.all_to_all(stale_values[0], 'patch', split_axis=1, concat_axis=0, til...  9.9 us
    all_to_all x1, waiting for transfers between devices, per_device(): lax.all_to_all(stale_keys[0], 'patch', split_axis=1, concat_axis=0, tiled...  9.43 us
    dot_general x1, matrix products, per_device(): jnp.dot(normed_every, lax.all_gather(query_columns, 'step', axis=0, tiled...  7.27 us
    convert_element_type x3, local copies, waits for them, and re-layouts, finish_heads(): jnp.transpose(blended, (1, 0, 2)).reshape(token_count, -1)  7.09 us
  transfers between devices with their start and end apart: 6, of which 5 were waited for; matrix products, arithmetic and copies ran while one was open for 16% of the time, Pallas kernels for 0%

commit v1 on v0

--- a/solution.py
+++ b/solution.py
@@ -1,8 +1,11 @@
+import functools
 import math
 
 import jax
 import jax.numpy as jnp
 from jax import lax
+from jax.experimental import pallas as pl
+from jax.experimental.pallas import tpu as pltpu
 from jax.sharding import PartitionSpec as P
 
 D = 3072
@@ -98,7 +101,7 @@
     return jnp.transpose(blended, (1, 0, 2)).reshape(token_count, -1).astype(jnp.bfloat16)
 
 
-def per_device(
+def plain_device(
     latent_old,
     noise_start,
     step_index,
@@ -164,6 +167,551 @@
     return result[None]
 
 
+NT = (((1,), (1,)), ((), ()))
+NN = (((1,), (0,)), ((), ()))
+
+
+def send(src, dst, send_sem, recv_sem, target):
+    return pltpu.make_async_remote_copy(
+        src_ref=src,
+        dst_ref=dst,
+        send_sem=send_sem,
+        recv_sem=recv_sem,
+        device_id=target,
+        device_id_type=pl.DeviceIdType.MESH,
+    )
+
+
+def dot(a, b, dims=NN):
+    return lax.dot_general(a, b, dims, preferred_element_type=jnp.float32)
+
+
+def fused_kernel(
+    sizes,
+    latent_ref,
+    noise_ref,
+    embedded_ref,
+    dt_ref,
+    embed_ref,
+    bias_ref,
+    gain_ref,
+    final_ref,
+    mod_hbm,
+    wq_hbm,
+    key_hbm,
+    value_hbm,
+    wo_hbm,
+    out_ref,
+    lat_all,
+    mod_buf,
+    mod_out,
+    wq_buf,
+    key_buf,
+    value_buf,
+    wo_buf,
+    normed,
+    raw,
+    queries,
+    att,
+    branch,
+    embed_mine,
+    bias_mine,
+    gate_mine,
+    final_mine,
+    pay,
+    pay_in,
+    drift_out,
+    drift_in,
+    local_sem,
+    lat_s,
+    lat_r,
+    kv_s,
+    kv_r,
+    wqz_s,
+    wqz_r,
+    wqy_s,
+    wqy_r,
+    woz_s,
+    woz_r,
+    woy_s,
+    woy_r,
+    att_s,
+    att_r,
+    pay_s,
+    pay_r,
+    dr_s,
+    dr_r,
+):
+    nr, ns, np_ = sizes
+    r, s, p = lax.axis_index("rep"), lax.axis_index("step"), lax.axis_index("patch")
+    tokens = latent_ref.shape[0]
+    total = tokens * np_
+    width = embed_ref.shape[1]
+    rows = wq_hbm.shape[0]
+    inner = wq_hbm.shape[1]
+    group = inner // np_
+    heads = group // HEAD
+    keys = key_hbm.shape[0]
+    half = rows // nr
+    mine = rows // np_
+    part = mine // nr
+    feats = width // np_
+
+    def patch_of(d):
+        return lax.rem(p + d, np_)
+
+    def step_of(d):
+        return lax.rem(s + d, ns)
+
+    def rep_of(d):
+        return lax.rem(r + d, nr)
+
+    loads = [
+        pltpu.make_async_copy(mod_hbm, mod_buf, local_sem.at[0]),
+        pltpu.make_async_copy(
+            wq_hbm.at[:, pl.ds(pl.multiple_of(p * group, HEAD), group)],
+            wq_buf.at[s],
+            local_sem.at[1],
+        ),
+        pltpu.make_async_copy(
+            key_hbm.at[:, pl.ds(pl.multiple_of(p * group, HEAD), group)],
+            key_buf.at[pl.ds(pl.multiple_of(p * keys, 16), keys), :],
+            local_sem.at[2],
+        ),
+        pltpu.make_async_copy(
+            value_hbm.at[:, pl.ds(pl.multiple_of(p * group, HEAD), group)],
+            value_buf.at[pl.ds(pl.multiple_of(p * keys, 16), keys), :],
+            local_sem.at[3],
+        ),
+        pltpu.make_async_copy(
+            wo_hbm.at[pl.ds(pl.multiple_of(p * mine, 16), mine), :],
+            wo_buf.at[pl.ds(pl.multiple_of(s * mine, 16), mine), :],
+            local_sem.at[4],
+        ),
+    ]
+    barrier = pltpu.get_barrier_semaphore()
+    for d in range(1, np_):
+        pl.semaphore_signal(
+            barrier, inc=1, device_id={"patch": patch_of(d)}, device_id_type=pl.DeviceIdType.MESH
+        )
+    for d in range(1, ns):
+        pl.semaphore_signal(
+            barrier, inc=1, device_id={"step": step_of(d)}, device_id_type=pl.DeviceIdType.MESH
+        )
+    for d in range(1, nr):
+        pl.semaphore_signal(
+            barrier, inc=1, device_id={"rep": rep_of(d)}, device_id_type=pl.DeviceIdType.MESH
+        )
+    for load in loads:
+        load.start()
+    pl.semaphore_wait(barrier, np_ - 1 + ns - 1 + nr - 1)
+
+    def lat_copy(d, owner):
+        return send(
+            latent_ref, lat_all.at[owner], lat_s.at[d], lat_r.at[d], {"patch": patch_of(d)}
+        )
+
+    def kv_copy(which, d, taker, owner):
+        source = (key_hbm, value_hbm)[which]
+        target = (key_buf, value_buf)[which]
+        return send(
+            source.at[:, pl.ds(pl.multiple_of(taker * group, HEAD), group)],
+            target.at[pl.ds(pl.multiple_of(owner * keys, 16), keys), :],
+            kv_s.at[which, d],
+            kv_r.at[which, d],
+            {"patch": taker},
+        )
+
+    def wqz_copy(d, owner):
+        return send(
+            wq_hbm.at[
+                pl.ds(pl.multiple_of(r * half, 16), half),
+                pl.ds(pl.multiple_of(p * group, HEAD), group),
+            ],
+            wq_buf.at[owner, pl.ds(pl.multiple_of(r * half, 16), half), :],
+            wqz_s.at[d],
+            wqz_r.at[d],
+            {"step": step_of(d)},
+        )
+
+    def wqy_copy(d, e, from_rep):
+        owner = step_of(ns - d)
+        spot = wq_buf.at[owner, pl.ds(pl.multiple_of(from_rep * half, 16), half), :]
+        return send(spot, spot, wqy_s.at[d, e], wqy_r.at[d, e], {"rep": rep_of(e)})
+
+    def woz_copy(d, owner):
+        return send(
+            wo_hbm.at[pl.ds(pl.multiple_of(p * mine + r * part, 16), part), :],
+            wo_buf.at[pl.ds(pl.multiple_of(owner * mine + r * part, 16), part), :],
+            woz_s.at[d],
+            woz_r.at[d],
+            {"step": step_of(d)},
+        )
+
+    def woy_copy(d, e, from_rep):
+        owner = step_of(ns - d)
+        spot = wo_buf.at[pl.ds(pl.multiple_of(owner * mine + from_rep * part, 16), part), :]
+        return send(spot, spot, woy_s.at[d, e], woy_r.at[d, e], {"rep": rep_of(e)})
+
+    for d in range(1, np_):
+        lat_copy(d, p).start()
+    order = [d for d in (1, ns - 1) if d > 0] + list(range(2, ns - 1))
+    order = list(dict.fromkeys(order))
+    for d in order:
+        wqz_copy(d, s).start()
+    for which in range(2):
+        for d in range(1, np_):
+            kv_copy(which, d, patch_of(d), p).start()
+    for d in order:
+        woz_copy(d, s).start()
+
+    loads[0].wait()
+    for block in range(3):
+        mod_out[:, block * width : (block + 1) * width] = dot(
+            embedded_ref[...], mod_buf[:, block * width : (block + 1) * width]
+        )
+
+    for k in range(np_):
+
+        @pl.when(p == k)
+        def _():
+            for z in range(ns):
+                start = z * rows + k * mine
+                spot = slice(z * mine, (z + 1) * mine)
+                embed_mine[:, spot] = embed_ref[:, start : start + mine]
+                bias_mine[:, spot] = bias_ref[:, start : start + mine]
+                gate_mine[:, spot] = mod_out[
+                    0:1, 2 * width + start : 2 * width + start + mine
+                ]
+                final_mine[spot, :] = final_ref[start : start + mine, :]
+
+    lat_all[p] = latent_ref[...]
+    for d in range(1, np_):
+        lat_copy(d, patch_of(np_ - d)).wait_recv()
+
+    small = min(128, tokens)
+
+    def norm_block(i, _):
+        at = i * small
+        owner = lax.div(at, tokens)
+        inside = pl.multiple_of(lax.rem(at, tokens), small)
+        latent = lat_all[owner, pl.ds(inside, small), :].astype(jnp.bfloat16)
+        hidden = dot(latent, embed_ref[...]) + bias_ref[...]
+        centered = hidden - jnp.mean(hidden, axis=-1, keepdims=True)
+        row_var = jnp.mean(centered * centered, axis=-1, keepdims=True)
+        unit = centered * lax.rsqrt(row_var + epsilon)
+        shifted = unit * (1.0 + mod_out[0:1, width : 2 * width]) + mod_out[0:1, 0:width]
+        normed[pl.ds(pl.multiple_of(at, small), small), :] = shifted.astype(jnp.bfloat16)
+        return 0
+
+    lax.fori_loop(0, total // small, norm_block, 0)
+
+    chunk = min(256, total)
+
+    def project(owner, start, depth, first):
+        def block(i, _):
+            at = pl.ds(pl.multiple_of(i * chunk, chunk), chunk)
+            lanes = pl.ds(pl.multiple_of(owner * rows + start, HEAD), depth)
+            term = dot(
+                normed[at, lanes],
+                wq_buf[owner, pl.ds(pl.multiple_of(start, 16), depth), :],
+            )
+            raw[at, :] = term if first else raw[at, :] + term
+            return 0
+
+        lax.fori_loop(0, total // chunk, block, 0)
+
+    loads[1].wait()
+    project(s, 0, rows, True)
+    for d in order:
+        owner = step_of(ns - d)
+        wqz_copy(d, owner).wait_recv()
+        for e in range(1, nr):
+            wqy_copy(d, e, r).start()
+        project(owner, r * half, half, False)
+    for d in order:
+        owner = step_of(ns - d)
+        for e in range(1, nr):
+            other = rep_of(nr - e)
+            wqy_copy(d, e, other).wait_recv()
+            project(owner, other * half, half, False)
+
+    def norm_query(i, _):
+        at = pl.ds(pl.multiple_of(i * chunk, chunk), chunk)
+        for h in range(heads):
+            q = raw[at, h * HEAD : (h + 1) * HEAD]
+            q = q * lax.rsqrt(jnp.mean(q * q, axis=-1, keepdims=True) + epsilon) * gain_ref[...]
+            queries[at, h * HEAD : (h + 1) * HEAD] = q.astype(jnp.bfloat16)
+        return 0
+
+    lax.fori_loop(0, total // chunk, norm_query, 0)
+
+    loads[2].wait()
+    loads[3].wait()
+    for which in range(2):
+        for d in range(1, np_):
+            kv_copy(which, d, p, patch_of(np_ - d)).wait_recv()
+
+    across = lax.rem(p + 2, np_)
+    beside = p + 1 - 2 * lax.rem(p, 2)
+    diagonal = lax.rem(beside + 2, np_)
+
+    def head_copy(way, h, owner):
+        spot = att.at[:, pl.ds(pl.multiple_of((owner * heads + h) * HEAD, HEAD), HEAD)]
+        return send(
+            spot,
+            spot,
+            att_s.at[way, h],
+            att_r.at[way, h],
+            {"patch": (across if way == 0 else beside)},
+        )
+
+    def pass_on(h):
+        head_copy(0, h, across).wait_recv()
+        head_copy(2, h, across).start()
+
+    factor = 1.0 / math.sqrt(HEAD)
+    for h in range(heads):
+
+        def attend(i, _):
+            at = pl.ds(pl.multiple_of(i * chunk, chunk), chunk)
+            lanes = slice(h * HEAD, (h + 1) * HEAD)
+            scores = dot(queries[at, lanes], key_buf[:, lanes], NT)
+            peak = jnp.max(scores, axis=-1, keepdims=True)
+            weights = jnp.exp((scores - peak) * factor)
+            row_total = jnp.sum(weights, axis=-1, keepdims=True)
+            blended = dot(weights.astype(jnp.bfloat16), value_buf[:, lanes]) / row_total
+            spot = pl.ds(pl.multiple_of((p * heads + h) * HEAD, HEAD), HEAD)
+            att[at, spot] = blended.astype(jnp.bfloat16)
+            return 0
+
+        lax.fori_loop(0, total // chunk, attend, 0)
+        head_copy(0, h, p).start()
+        head_copy(1, h, p).start()
+        if h >= 1:
+            pass_on(h - 1)
+
+    for d in order:
+        woz_copy(d, step_of(ns - d)).wait_recv()
+        for e in range(1, nr):
+            woy_copy(d, e, r).start()
+    for h in range(heads):
+        head_copy(1, h, beside).wait_recv()
+    loads[4].wait()
+    for d in order:
+        for e in range(1, nr):
+            woy_copy(d, e, rep_of(nr - e)).wait_recv()
+    pair = 2 * group
+    chip = lax.div(p, 2)
+    here = pl.ds(pl.multiple_of(chip * pair, HEAD), pair)
+    there = pl.ds(pl.multiple_of((1 - chip) * pair, HEAD), pair)
+
+    def near(i, _):
+        at = pl.ds(pl.multiple_of(i * chunk, chunk), chunk)
+        branch[at, :] = dot(att[at, here], wo_buf[:, here], NT)
+        return 0
+
+    lax.fori_loop(0, total // chunk, near, 0)
+    pass_on(heads - 1)
+    for h in range(heads):
+        head_copy(2, h, diagonal).wait_recv()
+
+    own_sum = jnp.sum(final_mine[...].astype(jnp.float32), axis=0, keepdims=True)
+    channels = final_ref.shape[1]
+
+    def finish(d):
+        owner = patch_of(d)
+        at = pl.ds(pl.multiple_of(owner * tokens, tokens), tokens)
+        full = branch[at, :] + dot(att[at, there], wo_buf[:, there], NT)
+        latent = lat_all[owner].astype(jnp.bfloat16)
+        hidden = dot(latent, embed_mine[...]) + bias_mine[...]
+        mixed = hidden + gate_mine[...] * full
+        middle = jnp.mean(mixed, axis=-1, keepdims=True)
+        centered = mixed - middle
+        spread = jnp.sum(centered * centered, axis=-1, keepdims=True)
+        lane = lax.broadcasted_iota(jnp.int32, (tokens, channels), 1)
+        pay[d, :, 0:channels] = (
+            dot(centered.astype(jnp.bfloat16), final_mine[...]) + middle * own_sum
+        )
+        pay[d, :, channels : 2 * channels] = jnp.where(lane < channels // 2, middle, spread)
+
+    def pay_copy(d):
+        return send(
+            pay.at[d], pay_in.at[d], pay_s.at[d], pay_r.at[d], {"patch": patch_of(d)}
+        )
+
+    def finish_other(d, _):
+        finish(d)
+        pay_copy(d).start()
+        return 0
+
+    lax.fori_loop(1, np_, finish_other, 0)
+    finish(0)
+    for d in range(1, np_):
+        pay_copy(d).wait_recv()
+    every = [pay[0]] + [pay_in[d] for d in range(1, np_)]
+    product = sum(item[:, 0:channels] for item in every)
+    middles = [item[:, channels : channels + 1] for item in every]
+    row_mean = sum(middles) / np_
+    spread = sum(
+        item[:, channels + channels // 2 : channels + channels // 2 + 1]
+        + feats * (middle - row_mean) * (middle - row_mean)
+        for item, middle in zip(every, middles)
+    )
+    all_sum = jnp.sum(final_ref[...].astype(jnp.float32), axis=0, keepdims=True)
+    velocity = (product - row_mean * all_sum) * lax.rsqrt(spread / width + epsilon)
+    drift = velocity * dt_ref[0:1, 0:1]
+    drift_out[...] = drift.astype(jnp.bfloat16)
+
+    def drift_copy(d):
+        return send(
+            drift_out, drift_in.at[d], dr_s.at[d], dr_r.at[d], {"step": step_of(d)}
+        )
+
+    for d in range(1, ns):
+
+        @pl.when(s + d < ns)
+        def _():
+            drift_copy(d).start()
+
+    out_ref[...] = noise_ref[...] + drift
+    for d in range(1, ns):
+
+        @pl.when(s - d >= 0)
+        def _():
+            drift_copy(d).wait_recv()
+            out_ref[...] += drift_in[d].astype(jnp.float32)
+
+    for d in range(1, np_):
+        lat_copy(d, p).wait_send()
+        pay_copy(d).wait_send()
+        for which in range(2):
+            kv_copy(which, d, patch_of(d), p).wait_send()
+    for d in range(1, ns):
+        wqz_copy(d, s).wait_send()
+        woz_copy(d, s).wait_send()
+        for e in range(1, nr):
+            wqy_copy(d, e, r).wait_send()
+            woy_copy(d, e, r).wait_send()
+
+        @pl.when(s + d < ns)
+        def _():
+            drift_copy(d).wait_send()
+
+    for h in range(heads):
+        head_copy(0, h, p).wait_send()
+        head_copy(1, h, p).wait_send()
+        head_copy(2, h, across).wait_send()
+
+
+def fused_device(
+    sizes,
+    latent_old,
+    noise_start,
+    step_index,
+    sigma_table,
+    mod_weight,
+    embed_weight,
+    embed_bias,
+    query_weight,
+    query_gain,
+    stale_keys,
+    stale_values,
+    out_weight,
+    final_weight,
+):
+    nr, ns, np_ = sizes
+    step_slot = step_index[0]
+    table_slots = jnp.arange(sigma_table.shape[0])
+    sigma_now = jnp.sum(jnp.where(table_slots == step_slot, sigma_table, 0.0))
+    sigma_next = jnp.sum(jnp.where(table_slots == step_slot + 1, sigma_table, 0.0))
+    embedded = jax.nn.silu(time_embed(sigma_now)).astype(jnp.bfloat16)
+    embedded = jnp.broadcast_to(embedded[None, :], (16, embedded.shape[0]))
+    dt = jnp.full((1, HEAD), sigma_next - sigma_now, jnp.float32)
+    tokens, channels = latent_old.shape[1:]
+    width = embed_weight.shape[1]
+    rows, inner = query_weight.shape
+    keys = stale_keys.shape[1]
+    group = inner // np_
+    heads = group // HEAD
+    feats = width // np_
+    total = tokens * np_
+    bf, f32 = jnp.bfloat16, jnp.float32
+    dma = pltpu.SemaphoreType.DMA
+    vmem = pl.BlockSpec(memory_space=pltpu.VMEM)
+    anywhere = pl.BlockSpec(memory_space=pl.ANY)
+    out = pl.pallas_call(
+        functools.partial(fused_kernel, sizes),
+        out_shape=jax.ShapeDtypeStruct((tokens, channels), f32),
+        in_specs=[vmem] * 8 + [anywhere] * 5,
+        out_specs=vmem,
+        scratch_shapes=[
+            pltpu.VMEM((np_, tokens, channels), f32),
+            pltpu.VMEM(mod_weight.shape, bf),
+            pltpu.VMEM((16, 3 * width), f32),
+            pltpu.VMEM((ns, rows, group), bf),
+            pltpu.VMEM((np_ * keys, group), bf),
+            pltpu.VMEM((np_ * keys, group), bf),
+            pltpu.VMEM((feats, inner), bf),
+            pltpu.VMEM((total, width), bf),
+            pltpu.VMEM((total, group), f32),
+            pltpu.VMEM((total, group), bf),
+            pltpu.VMEM((total, inner), bf),
+            pltpu.VMEM((total, feats), f32),
+            pltpu.VMEM((channels, feats), bf),
+            pltpu.VMEM((1, feats), f32),
+            pltpu.VMEM((1, feats), f32),
+            pltpu.VMEM((feats, channels), bf),
+            pltpu.VMEM((np_, tokens, 2 * channels), f32),
+            pltpu.VMEM((np_, tokens, 2 * channels), f32),
+            pltpu.VMEM((tokens, channels), bf),
+            pltpu.VMEM((ns, tokens, channels), bf),
+            dma((5,)),
+            dma((np_,)),
+            dma((np_,)),
+            dma((2, np_)),
+            dma((2, np_)),
+            dma((ns,)),
+            dma((ns,)),
+            dma((ns, nr)),
+            dma((ns, nr)),
+            dma((ns,)),
+            dma((ns,)),
+            dma((ns, nr)),
+            dma((ns, nr)),
+            dma((3, heads)),
+            dma((3, heads)),
+            dma((np_,)),
+            dma((np_,)),
+            dma((ns,)),
+            dma((ns,)),
+        ],
+        compiler_params=pltpu.CompilerParams(
+            collective_id=0, has_side_effects=True, vmem_limit_bytes=60 * 1024 * 1024
+        ),
+    )(
+        latent_old[0],
+        noise_start,
+        embedded,
+        dt,
+        embed_weight,
+        embed_bias[None, :],
+        query_gain[None, :],
+        final_weight,
+        mod_weight,
+        query_weight,
+        stale_keys[0],
+        stale_values[0],
+        out_weight,
+    )
+    return out[None]
+
+
+def fits(mesh):
+    nr, ns, np_ = (mesh.shape[axis] for axis in ("rep", "step", "patch"))
+    return np_ == 4 and ns <= 8 and D % (ns * np_ * nr * 16) == 0 and D // (ns * nr) % HEAD == 0
+
+
 def solution(mesh):
     placed = (
         P(("rep", "step"), "patch", None),
@@ -180,6 +728,8 @@
         P("step", None),
         P(),
     )
+    sizes = tuple(mesh.shape[axis] for axis in ("rep", "step", "patch"))
+    per_device = functools.partial(fused_device, sizes) if fits(mesh) else plain_device
     return jax.shard_map(
         per_device,
         mesh=mesh,

time: 307 us -> 112 us (0.36)
  waiting for transfers between devices: 197 us -> 0 us
  Pallas kernels: 0 us -> 97.8 us
  matrix products: 25 us -> 0 us
  local copies, waits for them, and re-layouts: 32.3 us -> 8.14 us
  blocking collectives: 13.6 us -> 0 us
  between operations: 15.9 us -> 2.48 us
  starting transfers between devices: 12.9 us -> 0 us
  other arithmetic: 9.39 us -> 1.43 us
    all_gather x3 -> x0, waiting for transfers between devices: 166 us -> none  [the longest x1 121 us: per_device(): lax.all_gather(out_weight, 'step', axis=0, tiled=True)]
    pallas_call x0 -> x1, Pallas kernels: none -> 97.8 us  [fused_device(): pl.pallas_call(functools.partial(fused_kernel, sizes), out_shape=jax.Shap...]
    all_to_all x3 -> x0, waiting for transfers between devices: 29.6 us -> none  [the longest x1 10.3 us: per_device(): lax.all_to_all(attended_every, 'patch', split_axis=0, concat_axis=1, tile...]
    dot_general x7 -> x0, matrix products: 25 us -> none  [the longest x1 7.27 us: per_device(): jnp.dot(normed_every, lax.all_gather(query_columns, 'step', axis=0, tiled...]
    all_gather x1 -> x0, blocking collectives: 13.6 us -> none  [entering(): gathered = lax.all_gather(shard.astype(jnp.bfloat16), axis)]
    all_to_all x3 -> x0, starting transfers between devices: 12.8 us -> none  [the longest x1 4.41 us: per_device(): lax.all_to_all(stale_values[0], 'patch', split_axis=1, concat_axis=0, til...]
    reshape x5 -> x0, local copies, waits for them, and re-layouts: 10.8 us -> none  [the longest x1 3.71 us: attend_block(): key_split = key_piece.reshape(row_count, head_count, HEAD)]
    all_to_all x4 -> x0, local copies, waits for them, and re-layouts: 10 us -> none  [the longest x2 5.06 us: per_device(): lax.all_to_all(stale_keys[0], 'patch', split_axis=1, concat_axis=0, tiled...]
  transfers between devices with their start and end apart: 6 -> 0, of which waited for: 5 -> 0; matrix products, arithmetic and copies ran while one was open for 16% -> 0% of each run, Pallas kernels for 0% -> 0%
where the time goes in v1:
time: 112 us; the launch traced here: 110 us
  Pallas kernels  97.8 us (87%)
  local copies, waits for them, and re-layouts  8.14 us (7%)
  between operations  2.48 us (2%)
  other arithmetic  1.43 us (1%)
    pallas_call x1, Pallas kernels, fused_device(): pl.pallas_call(functools.partial(fused_kernel, sizes), out_shape=jax.Shap...  97.8 us
    unnamed x3, local copies, waits for them, and re-layouts  5.34 us

profile of v1, /device:TPU:0, one launch (start us, length us, event | category | flops | bytes accessed | tf_op | source)
XLA Modules:
  0.0 109.9 jit_solution(18160082620222049499)
XLA Ops:
  0.7 1.4 %select_reduce_fusion = (f32[]{:T(128)}, f32[]{:T(128)}) fusion(f32[1000]{0:T(1024)} %param.16, s32[]{:T(128)S(6)} %add.12, s32[]{:T(128)} %bitcast.7), kind=kLoop, calls=%fused_computation | loop fusion | flops 5998 | bytes 4016 | tf_op jit(solution)/shard_map/reduce_sum | solution.py:627
  3.8 0.6 broadcast_in_dim.25.dt_ref
  4.5 0.6 broadcast_in_dim.24.embedded_ref
  5.1 1.6 %copy.14 = f32[1,256,64]{2,1,0:T(8,128)} copy(f32[1,256,64]{1,2,0:T(8,128)} %param.13) | data formatting | bytes 131072 | tf_op args[0]
  6.7 1.6 %copy.15.noise_ref = f32[256,64]{1,0:T(8,128)} copy(f32[256,64]{0,1:T(8,128)} %param.14) | data formatting | bytes 131072 | tf_op args[1]
  8.3 2.1 %copy.16.final_ref = bf16[3072,64]{1,0:T(8,128)(2,1)} copy(bf16[3072,64]{0,1:T(8,128)(2,1)} %param.25) | data formatting | bytes 786432 | tf_op args[12]
  10.4 97.8 %shard_map.127 = f32[256,64]{1,0:T(8,128)} custom-call(f32[256,64]{1,0:T(8,128)} %bitcast.12, f32[256,64]{1,0:T(8,128)} %copy.15.noise_ref, bf16[16,256]{1,0:T(8,128)(2,1)} %broadcast_in_dim.24.embedded_ref, f32[1,128]{1,0:T(1,128)} %broadcast_in_dim.25.dt_ref, bf16[64,3072]{1,0:T(8,128)(2,1)} %embed_ref.1, f32[1,3072]{1,0:T(1,128)} %bitcast.13, ...), custom_call_target="tpu_custom_call" | custom-call | tf_op jit(solution)/shard_map/pallas_call | solution.py:643
  108.3 1.6 %copy.17 = f32[1,256,64]{1,2,0:T(8,128)} copy(f32[1,256,64]{2,1,0:T(8,128)} %bitcast.11) | data formatting | bytes 131072 | tf_op jit(solution)/shard_map/broadcast_in_dim | solution.py:707
  (2 shorter events, 0.1 us)

commit v2 on v1

--- a/solution.py
+++ b/solution.py
@@ -222,6 +222,7 @@
     pay_in,
     drift_out,
     drift_in,
+    drift_sum,
     local_sem,
     lat_s,
     lat_r,
@@ -244,7 +245,7 @@
 ):
     nr, ns, np_ = sizes
     r, s, p = lax.axis_index("rep"), lax.axis_index("step"), lax.axis_index("patch")
-    tokens = latent_ref.shape[0]
+    channels, tokens = latent_ref.shape
     total = tokens * np_
     width = embed_ref.shape[1]
     rows = wq_hbm.shape[0]
@@ -355,16 +356,55 @@
 
     for d in range(1, np_):
         lat_copy(d, p).start()
-    order = [d for d in (1, ns - 1) if d > 0] + list(range(2, ns - 1))
-    order = list(dict.fromkeys(order))
-    for d in order:
-        wqz_copy(d, s).start()
+    relayed = ns == 4
+    if relayed:
+        early = 3 - 2 * jnp.minimum(s, 1)
+        order = [2, early, 4 - early]
+    else:
+        order = list(range(1, ns))
+
+    def start_direct(copy):
+        for d in [2, 1, 3] if relayed else order:
+            if relayed and d != 2:
+
+                @pl.when(s != (0 if d == 3 else ns - 1))
+                def _():
+                    copy(d, s).start()
+
+            else:
+                copy(d, s).start()
+
+    def direct_sent(copy):
+        for d in range(1, ns):
+            if relayed and d != 2:
+
+                @pl.when(s != (0 if d == 3 else ns - 1))
+                def _():
+                    copy(d, s).wait_send()
+
+            else:
+                copy(d, s).wait_send()
+
+    def relay(spot, send_sem, recv_sem, act):
+        if relayed:
+            for place, target, d in ((2, 3, 3), (1, 0, 1)):
+
+                @pl.when(s == place)
+                def _():
+                    act(send(spot, spot, send_sem.at[0], recv_sem.at[d], {"step": target}))
+
+    def wq_relay(act):
+        spot = wq_buf.at[step_of(ns - 2), pl.ds(pl.multiple_of(r * half, 16), half), :]
+        relay(spot, wqz_s, wqz_r, act)
+
+    def wo_relay(act):
+        at = pl.multiple_of(step_of(ns - 2) * mine + r * part, 16)
+        relay(wo_buf.at[pl.ds(at, part), :], woz_s, woz_r, act)
+
+    start_direct(wqz_copy)
     for which in range(2):
         for d in range(1, np_):
             kv_copy(which, d, patch_of(d), p).start()
-    for d in order:
-        woz_copy(d, s).start()
-
     loads[0].wait()
     for block in range(3):
         mod_out[:, block * width : (block + 1) * width] = dot(
@@ -383,7 +423,7 @@
                 gate_mine[:, spot] = mod_out[
                     0:1, 2 * width + start : 2 * width + start + mine
                 ]
-                final_mine[spot, :] = final_ref[start : start + mine, :]
+                final_mine[:, spot] = final_ref[:, start : start + mine]
 
     lat_all[p] = latent_ref[...]
     for d in range(1, np_):
@@ -395,7 +435,7 @@
         at = i * small
         owner = lax.div(at, tokens)
         inside = pl.multiple_of(lax.rem(at, tokens), small)
-        latent = lat_all[owner, pl.ds(inside, small), :].astype(jnp.bfloat16)
+        latent = lat_all[owner, :, pl.ds(inside, small)].T.astype(jnp.bfloat16)
         hidden = dot(latent, embed_ref[...]) + bias_ref[...]
         centered = hidden - jnp.mean(hidden, axis=-1, keepdims=True)
         row_var = jnp.mean(centered * centered, axis=-1, keepdims=True)
@@ -426,6 +466,9 @@
     for d in order:
         owner = step_of(ns - d)
         wqz_copy(d, owner).wait_recv()
+        if d is order[0]:
+            wq_relay(lambda copy: copy.start())
+            start_direct(woz_copy)
         for e in range(1, nr):
             wqy_copy(d, e, r).start()
         project(owner, r * half, half, False)
@@ -469,6 +512,13 @@
     def pass_on(h):
         head_copy(0, h, across).wait_recv()
         head_copy(2, h, across).start()
+
+    def wo_pass(d):
+        woz_copy(d, step_of(ns - d)).wait_recv()
+        if d is order[0]:
+            wo_relay(lambda copy: copy.start())
+        for e in range(1, nr):
+            woy_copy(d, e, r).start()
 
     factor = 1.0 / math.sqrt(HEAD)
     for h in range(heads):
@@ -490,11 +540,12 @@
         head_copy(1, h, p).start()
         if h >= 1:
             pass_on(h - 1)
-
-    for d in order:
-        woz_copy(d, step_of(ns - d)).wait_recv()
-        for e in range(1, nr):
-            woy_copy(d, e, r).start()
+        if h == heads - 2:
+            wo_pass(order[0])
+
+    for d in order[1:]:
+        wo_pass(d)
+    pass_on(heads - 1)
     for h in range(heads):
         head_copy(1, h, beside).wait_recv()
     loads[4].wait()
@@ -512,18 +563,19 @@
         return 0
 
     lax.fori_loop(0, total // chunk, near, 0)
-    pass_on(heads - 1)
     for h in range(heads):
         head_copy(2, h, diagonal).wait_recv()
 
-    own_sum = jnp.sum(final_mine[...].astype(jnp.float32), axis=0, keepdims=True)
-    channels = final_ref.shape[1]
+    own_sum = dot(jnp.ones((16, feats), jnp.bfloat16), final_mine[...], NT)[0:1]
+
+    def partner(d):
+        return jnp.where(d == 1, across, jnp.where(d == 2, diagonal, jnp.where(d == 3, beside, p)))
 
     def finish(d):
-        owner = patch_of(d)
+        owner = partner(d)
         at = pl.ds(pl.multiple_of(owner * tokens, tokens), tokens)
         full = branch[at, :] + dot(att[at, there], wo_buf[:, there], NT)
-        latent = lat_all[owner].astype(jnp.bfloat16)
+        latent = lat_all[owner].T.astype(jnp.bfloat16)
         hidden = dot(latent, embed_mine[...]) + bias_mine[...]
         mixed = hidden + gate_mine[...] * full
         middle = jnp.mean(mixed, axis=-1, keepdims=True)
@@ -531,13 +583,13 @@
         spread = jnp.sum(centered * centered, axis=-1, keepdims=True)
         lane = lax.broadcasted_iota(jnp.int32, (tokens, channels), 1)
         pay[d, :, 0:channels] = (
-            dot(centered.astype(jnp.bfloat16), final_mine[...]) + middle * own_sum
+            dot(centered.astype(jnp.bfloat16), final_mine[...], NT) + middle * own_sum
         )
         pay[d, :, channels : 2 * channels] = jnp.where(lane < channels // 2, middle, spread)
 
     def pay_copy(d):
         return send(
-            pay.at[d], pay_in.at[d], pay_s.at[d], pay_r.at[d], {"patch": patch_of(d)}
+            pay.at[d], pay_in.at[d], pay_s.at[d], pay_r.at[d], {"patch": partner(d)}
         )
 
     def finish_other(d, _):
@@ -558,7 +610,7 @@
         + feats * (middle - row_mean) * (middle - row_mean)
         for item, middle in zip(every, middles)
     )
-    all_sum = jnp.sum(final_ref[...].astype(jnp.float32), axis=0, keepdims=True)
+    all_sum = dot(jnp.ones((16, width), jnp.bfloat16), final_ref[...], NT)[0:1]
     velocity = (product - row_mean * all_sum) * lax.rsqrt(spread / width + epsilon)
     drift = velocity * dt_ref[0:1, 0:1]
     drift_out[...] = drift.astype(jnp.bfloat16)
@@ -574,22 +626,26 @@
         def _():
             drift_copy(d).start()
 
-    out_ref[...] = noise_ref[...] + drift
+    drift_sum[...] = drift
     for d in range(1, ns):
 
         @pl.when(s - d >= 0)
         def _():
             drift_copy(d).wait_recv()
-            out_ref[...] += drift_in[d].astype(jnp.float32)
+            drift_sum[...] += drift_in[d].astype(jnp.float32)
+
+    out_ref[...] = noise_ref[...] + drift_sum[...].T
 
     for d in range(1, np_):
         lat_copy(d, p).wait_send()
         pay_copy(d).wait_send()
         for which in range(2):
             kv_copy(which, d, patch_of(d), p).wait_send()
+    direct_sent(wqz_copy)
+    direct_sent(woz_copy)
+    wq_relay(lambda copy: copy.wait_send())
+    wo_relay(lambda copy: copy.wait_send())
     for d in range(1, ns):
-        wqz_copy(d, s).wait_send()
-        woz_copy(d, s).wait_send()
         for e in range(1, nr):
             wqy_copy(d, e, r).wait_send()
             woy_copy(d, e, r).wait_send()
@@ -642,11 +698,11 @@
     anywhere = pl.BlockSpec(memory_space=pl.ANY)
     out = pl.pallas_call(
         functools.partial(fused_kernel, sizes),
-        out_shape=jax.ShapeDtypeStruct((tokens, channels), f32),
+        out_shape=jax.ShapeDtypeStruct((channels, tokens), f32),
         in_specs=[vmem] * 8 + [anywhere] * 5,
         out_specs=vmem,
         scratch_shapes=[
-            pltpu.VMEM((np_, tokens, channels), f32),
+            pltpu.VMEM((np_, channels, tokens), f32),
             pltpu.VMEM(mod_weight.shape, bf),
             pltpu.VMEM((16, 3 * width), f32),
             pltpu.VMEM((ns, rows, group), bf),
@@ -661,11 +717,12 @@
             pltpu.VMEM((channels, feats), bf),
             pltpu.VMEM((1, feats), f32),
             pltpu.VMEM((1, feats), f32),
-            pltpu.VMEM((feats, channels), bf),
+            pltpu.VMEM((channels, feats), bf),
             pltpu.VMEM((np_, tokens, 2 * channels), f32),
             pltpu.VMEM((np_, tokens, 2 * channels), f32),
             pltpu.VMEM((tokens, channels), bf),
             pltpu.VMEM((ns, tokens, channels), bf),
+            pltpu.VMEM((tokens, channels), f32),
             dma((5,)),
             dma((np_,)),
             dma((np_,)),
@@ -690,26 +747,26 @@
             collective_id=0, has_side_effects=True, vmem_limit_bytes=60 * 1024 * 1024
         ),
     )(
-        latent_old[0],
-        noise_start,
+        latent_old[0].T,
+        noise_start.T,
         embedded,
         dt,
         embed_weight,
         embed_bias[None, :],
         query_gain[None, :],
-        final_weight,
+        final_weight.T,
         mod_weight,
         query_weight,
         stale_keys[0],
         stale_values[0],
         out_weight,
     )
-    return out[None]
+    return out.T[None]
 
 
 def fits(mesh):
     nr, ns, np_ = (mesh.shape[axis] for axis in ("rep", "step", "patch"))
-    return np_ == 4 and ns <= 8 and D % (ns * np_ * nr * 16) == 0 and D // (ns * nr) % HEAD == 0
+    return np_ == 4 and ns <= 4 and D % (ns * np_ * nr * 16) == 0 and D // (ns * nr) % HEAD == 0
 
 
 def solution(mesh):

time: 112 us -> 95.9 us (0.86)
  Pallas kernels: 97.8 us -> 87.6 us
  local copies, waits for them, and re-layouts: 8.14 us -> 2.63 us
    pallas_call x1, Pallas kernels: 97.8 us -> 87.6 us  [fused_device(): pl.pallas_call(functools.partial(fused_kernel, sizes), out_shape=jax.Shap...]
    unnamed x3 -> x1, local copies, waits for them, and re-layouts: 5.34 us -> 1.47 us
    broadcast_in_dim x1 -> x0, local copies, waits for them, and re-layouts: 1.62 us -> none  [fused_device(): return out[None]]
where the time goes in v2:
time: 95.9 us; the launch traced here: 94.2 us
  Pallas kernels  87.6 us (91%)
  local copies, waits for them, and re-layouts  2.63 us (3%)
  between operations  2.48 us (3%)
  other arithmetic  1.43 us (1%)
    pallas_call x1, Pallas kernels, fused_device(): pl.pallas_call(functools.partial(fused_kernel, sizes), out_shape=jax.Shap...  87.6 us

profile of v2, /device:TPU:0, one launch (start us, length us, event | category | flops | bytes accessed | tf_op | source)
XLA Modules:
  0.0 94.2 jit_solution(7543257996518732194)
XLA Ops:
  0.7 1.4 %select_reduce_fusion = (f32[]{:T(128)}, f32[]{:T(128)}) fusion(f32[1000]{0:T(1024)} %param.16, s32[]{:T(128)S(6)} %add.12, s32[]{:T(128)} %bitcast.13), kind=kLoop, calls=%fused_computation | loop fusion | flops 5998 | bytes 4016 | tf_op jit(solution)/shard_map/reduce_sum | solution.py:683
  3.8 0.5 broadcast_in_dim.25.dt_ref
  4.5 0.6 broadcast_in_dim.24.embedded_ref
  5.1 87.6 %shard_map.127 = f32[64,256]{1,0:T(8,128)} custom-call(f32[64,256]{1,0:T(8,128)} %bitcast.19, f32[64,256]{1,0:T(8,128)} %bitcast.20, bf16[16,256]{1,0:T(8,128)(2,1)} %broadcast_in_dim.24.embedded_ref, f32[1,128]{1,0:T(1,128)} %broadcast_in_dim.25.dt_ref, bf16[64,3072]{1,0:T(8,128)(2,1)} %embed_ref.1, f32[1,3072]{1,0:T(1,128)} %bitcast.21, ...), custom_call_target="tpu_custom_call" | custom-call | tf_op jit(solution)/shard_map/pallas_call | solution.py:699
  92.7 1.5 %copy.16 = f32[1,256,64]{1,2,0:T(8,128)} copy(f32[1,256,64]{1,2,0:T(8,128)} %bitcast.18) | data formatting | bytes 131072
  (2 shorter events, 0.1 us)

commit v3 on v2

--- a/solution.py
+++ b/solution.py
@@ -15,6 +15,7 @@
 
 
 epsilon = 1e-06
+CUTS = 2
 
 
 def entering(shard, axis, join, neutral):
@@ -257,6 +258,9 @@
     mine = rows // np_
     part = mine // nr
     feats = width // np_
+    cuts = CUTS
+    half_cut = half // cuts
+    part_cut = part // cuts
 
     def patch_of(d):
         return lax.rem(p + d, np_)
@@ -323,36 +327,37 @@
             {"patch": taker},
         )
 
-    def wqz_copy(d, owner):
+    def wq_rows(from_rep, c):
+        return pl.ds(pl.multiple_of(from_rep * half + c * half_cut, 16), half_cut)
+
+    def wo_rows(base, from_rep, c):
+        return pl.ds(pl.multiple_of(base * mine + from_rep * part + c * part_cut, 16), part_cut)
+
+    def wqz_copy(d, owner, c):
         return send(
-            wq_hbm.at[
-                pl.ds(pl.multiple_of(r * half, 16), half),
-                pl.ds(pl.multiple_of(p * group, HEAD), group),
-            ],
-            wq_buf.at[owner, pl.ds(pl.multiple_of(r * half, 16), half), :],
-            wqz_s.at[d],
-            wqz_r.at[d],
+            wq_hbm.at[wq_rows(r, c), pl.ds(pl.multiple_of(p * group, HEAD), group)],
+            wq_buf.at[owner, wq_rows(r, c), :],
+            wqz_s.at[d, c],
+            wqz_r.at[d, c],
             {"step": step_of(d)},
         )
 
-    def wqy_copy(d, e, from_rep):
-        owner = step_of(ns - d)
-        spot = wq_buf.at[owner, pl.ds(pl.multiple_of(from_rep * half, 16), half), :]
-        return send(spot, spot, wqy_s.at[d, e], wqy_r.at[d, e], {"rep": rep_of(e)})
-
-    def woz_copy(d, owner):
+    def wqy_copy(d, e, from_rep, c):
+        spot = wq_buf.at[step_of(ns - d), wq_rows(from_rep, c), :]
+        return send(spot, spot, wqy_s.at[d, e, c], wqy_r.at[d, e, c], {"rep": rep_of(e)})
+
+    def woz_copy(d, owner, c):
         return send(
-            wo_hbm.at[pl.ds(pl.multiple_of(p * mine + r * part, 16), part), :],
-            wo_buf.at[pl.ds(pl.multiple_of(owner * mine + r * part, 16), part), :],
-            woz_s.at[d],
-            woz_r.at[d],
+            wo_hbm.at[wo_rows(p, r, c), :],
+            wo_buf.at[wo_rows(owner, r, c), :],
+            woz_s.at[d, c],
+            woz_r.at[d, c],
             {"step": step_of(d)},
         )
 
-    def woy_copy(d, e, from_rep):
-        owner = step_of(ns - d)
-        spot = wo_buf.at[pl.ds(pl.multiple_of(owner * mine + from_rep * part, 16), part), :]
-        return send(spot, spot, woy_s.at[d, e], woy_r.at[d, e], {"rep": rep_of(e)})
+    def woy_copy(d, e, from_rep, c):
+        spot = wo_buf.at[wo_rows(step_of(ns - d), from_rep, c), :]
+        return send(spot, spot, woy_s.at[d, e, c], woy_r.at[d, e, c], {"rep": rep_of(e)})
 
     for d in range(1, np_):
         lat_copy(d, p).start()
@@ -363,52 +368,47 @@
     else:
         order = list(range(1, ns))
 
-    def start_direct(copy):
+    def each_direct(copy, act):
         for d in [2, 1, 3] if relayed else order:
-            if relayed and d != 2:
-
-                @pl.when(s != (0 if d == 3 else ns - 1))
-                def _():
-                    copy(d, s).start()
-
-            else:
-                copy(d, s).start()
-
-    def direct_sent(copy):
-        for d in range(1, ns):
-            if relayed and d != 2:
-
-                @pl.when(s != (0 if d == 3 else ns - 1))
-                def _():
-                    copy(d, s).wait_send()
-
-            else:
-                copy(d, s).wait_send()
-
-    def relay(spot, send_sem, recv_sem, act):
+            for c in range(cuts):
+                if relayed and d != 2:
+
+                    @pl.when(s != (0 if d == 3 else ns - 1))
+                    def _():
+                        act(copy(d, s, c))
+
+                else:
+                    act(copy(d, s, c))
+
+    def relay(spot, send_sem, recv_sem, c, act):
         if relayed:
             for place, target, d in ((2, 3, 3), (1, 0, 1)):
 
                 @pl.when(s == place)
                 def _():
-                    act(send(spot, spot, send_sem.at[0], recv_sem.at[d], {"step": target}))
-
-    def wq_relay(act):
-        spot = wq_buf.at[step_of(ns - 2), pl.ds(pl.multiple_of(r * half, 16), half), :]
-        relay(spot, wqz_s, wqz_r, act)
-
-    def wo_relay(act):
-        at = pl.multiple_of(step_of(ns - 2) * mine + r * part, 16)
-        relay(wo_buf.at[pl.ds(at, part), :], woz_s, woz_r, act)
-
-    start_direct(wqz_copy)
+                    act(send(spot, spot, send_sem.at[0, c], recv_sem.at[d, c], {"step": target}))
+
+    def wq_relay(c, act):
+        relay(wq_buf.at[step_of(ns - 2), wq_rows(r, c), :], wqz_s, wqz_r, c, act)
+
+    def wo_relay(c, act):
+        relay(wo_buf.at[wo_rows(step_of(ns - 2), r, c), :], woz_s, woz_r, c, act)
+
+    def begin(copy):
+        copy.start()
+
+    def sent(copy):
+        copy.wait_send()
+
+    each_direct(wqz_copy, begin)
     for which in range(2):
         for d in range(1, np_):
             kv_copy(which, d, patch_of(d), p).start()
     loads[0].wait()
+    embedded = jnp.broadcast_to(embedded_ref[...], (16, embedded_ref.shape[1])).astype(jnp.bfloat16)
     for block in range(3):
         mod_out[:, block * width : (block + 1) * width] = dot(
-            embedded_ref[...], mod_buf[:, block * width : (block + 1) * width]
+            embedded, mod_buf[:, block * width : (block + 1) * width]
         )
 
     for k in range(np_):
@@ -465,18 +465,21 @@
     project(s, 0, rows, True)
     for d in order:
         owner = step_of(ns - d)
-        wqz_copy(d, owner).wait_recv()
+        for c in range(cuts):
+            wqz_copy(d, owner, c).wait_recv()
+            if d is order[0]:
+                wq_relay(c, begin)
+            for e in range(1, nr):
+                wqy_copy(d, e, r, c).start()
         if d is order[0]:
-            wq_relay(lambda copy: copy.start())
-            start_direct(woz_copy)
-        for e in range(1, nr):
-            wqy_copy(d, e, r).start()
+            each_direct(woz_copy, begin)
         project(owner, r * half, half, False)
     for d in order:
         owner = step_of(ns - d)
         for e in range(1, nr):
             other = rep_of(nr - e)
-            wqy_copy(d, e, other).wait_recv()
+            for c in range(cuts):
+                wqy_copy(d, e, other, c).wait_recv()
             project(owner, other * half, half, False)
 
     def norm_query(i, _):
@@ -514,11 +517,12 @@
         head_copy(2, h, across).start()
 
     def wo_pass(d):
-        woz_copy(d, step_of(ns - d)).wait_recv()
-        if d is order[0]:
-            wo_relay(lambda copy: copy.start())
-        for e in range(1, nr):
-            woy_copy(d, e, r).start()
+        for c in range(cuts):
+            woz_copy(d, step_of(ns - d), c).wait_recv()
+            if d is order[0]:
+                wo_relay(c, begin)
+            for e in range(1, nr):
+                woy_copy(d, e, r, c).start()
 
     factor = 1.0 / math.sqrt(HEAD)
     for h in range(heads):
@@ -540,7 +544,7 @@
         head_copy(1, h, p).start()
         if h >= 1:
             pass_on(h - 1)
-        if h == heads - 2:
+        if h == 0:
             wo_pass(order[0])
 
     for d in order[1:]:
@@ -551,7 +555,8 @@
     loads[4].wait()
     for d in order:
         for e in range(1, nr):
-            woy_copy(d, e, rep_of(nr - e)).wait_recv()
+            for c in range(cuts):
+                woy_copy(d, e, rep_of(nr - e), c).wait_recv()
     pair = 2 * group
     chip = lax.div(p, 2)
     here = pl.ds(pl.multiple_of(chip * pair, HEAD), pair)
@@ -641,14 +646,16 @@
         pay_copy(d).wait_send()
         for which in range(2):
             kv_copy(which, d, patch_of(d), p).wait_send()
-    direct_sent(wqz_copy)
-    direct_sent(woz_copy)
-    wq_relay(lambda copy: copy.wait_send())
-    wo_relay(lambda copy: copy.wait_send())
+    each_direct(wqz_copy, sent)
+    each_direct(woz_copy, sent)
+    for c in range(cuts):
+        wq_relay(c, sent)
+        wo_relay(c, sent)
     for d in range(1, ns):
         for e in range(1, nr):
-            wqy_copy(d, e, r).wait_send()
-            woy_copy(d, e, r).wait_send()
+            for c in range(cuts):
+                wqy_copy(d, e, r, c).wait_send()
+                woy_copy(d, e, r, c).wait_send()
 
         @pl.when(s + d < ns)
         def _():
@@ -682,8 +689,8 @@
     sigma_now = jnp.sum(jnp.where(table_slots == step_slot, sigma_table, 0.0))
     sigma_next = jnp.sum(jnp.where(table_slots == step_slot + 1, sigma_table, 0.0))
     embedded = jax.nn.silu(time_embed(sigma_now)).astype(jnp.bfloat16)
-    embedded = jnp.broadcast_to(embedded[None, :], (16, embedded.shape[0]))
-    dt = jnp.full((1, HEAD), sigma_next - sigma_now, jnp.float32)
+    embedded = embedded.astype(jnp.float32)[None, :]
+    dt = (sigma_next - sigma_now).reshape(1, 1)
     tokens, channels = latent_old.shape[1:]
     width = embed_weight.shape[1]
     rows, inner = query_weight.shape
@@ -728,14 +735,14 @@
             dma((np_,)),
             dma((2, np_)),
             dma((2, np_)),
-            dma((ns,)),
-            dma((ns,)),
-            dma((ns, nr)),
-            dma((ns, nr)),
-            dma((ns,)),
-            dma((ns,)),
-            dma((ns, nr)),
-            dma((ns, nr)),
+            dma((ns, CUTS)),
+            dma((ns, CUTS)),
+            dma((ns, nr, CUTS)),
+            dma((ns, nr, CUTS)),
+            dma((ns, CUTS)),
+            dma((ns, CUTS)),
+            dma((ns, nr, CUTS)),
+            dma((ns, nr, CUTS)),
             dma((3, heads)),
             dma((3, heads)),
             dma((np_,)),
@@ -766,7 +773,7 @@
 
 def fits(mesh):
     nr, ns, np_ = (mesh.shape[axis] for axis in ("rep", "step", "patch"))
-    return np_ == 4 and ns <= 4 and D % (ns * np_ * nr * 16) == 0 and D // (ns * nr) % HEAD == 0
+    return np_ == 4 and ns <= 4 and D % (ns * np_ * nr * CUTS * 16) == 0 and D // (ns * nr) % HEAD == 0
 
 
 def solution(mesh):

time: 95.9 us -> 97.9 us (1.021)
  Pallas kernels: 87.6 us -> 90.6 us
  local copies, waits for them, and re-layouts: 2.63 us -> 1.47 us
    pallas_call x1, Pallas kernels: 87.6 us -> 90.6 us  [fused_device(): pl.pallas_call(functools.partial(fused_kernel, sizes), out_shape=jax.Shap...]
    broadcast_in_dim x2 -> x0, local copies, waits for them, and re-layouts: 1.16 us -> none  [the longest x1 0.62 us: fused_device(): embedded = jnp.broadcast_to(embedded[None, :], (16, embedded.shape[0]))]
where the time goes in v3:
time: 97.9 us; the launch traced here: 96.5 us
  Pallas kernels  90.6 us (93%)
  between operations  2.48 us (3%)
  other arithmetic  2.01 us (2%)
  local copies, waits for them, and re-layouts  1.47 us (2%)
    pallas_call x1, Pallas kernels, fused_device(): pl.pallas_call(functools.partial(fused_kernel, sizes), out_shape=jax.Shap...  90.6 us

profile of v3, /device:TPU:0, one launch (start us, length us, event | category | flops | bytes accessed | tf_op | source)
XLA Modules:
  0.0 96.5 jit_solution(14195174235313480543)
XLA Ops:
  0.7 1.4 %select_reduce_fusion = (f32[]{:T(128)}, f32[]{:T(128)}) fusion(f32[1000]{0:T(1024)} %param.16, s32[]{:T(128)S(6)} %add.15, s32[]{:T(128)} %bitcast.18), kind=kLoop, calls=%fused_computation | loop fusion | flops 5998 | bytes 4016 | tf_op jit(solution)/shard_map/reduce_sum | solution.py:690
  3.9 0.6 convert_convert_fusion.embedded_ref
  4.5 90.6 %shard_map.127 = f32[64,256]{1,0:T(8,128)} custom-call(f32[64,256]{1,0:T(8,128)} %bitcast.24, f32[64,256]{1,0:T(8,128)} %bitcast.25, f32[1,256]{1,0:T(1,128)} %convert_convert_fusion.embedded_ref, f32[1,1]{1,0:T(1,128)} %bitcast.6.dt_ref, bf16[64,3072]{1,0:T(8,128)(2,1)} %embed_ref.1, f32[1,3072]{1,0:T(1,128)} %bitcast.26, f32[1,128]{1,0:T(1,128)} %bitcast.27, ...), custom_call_target="tpu_custom_call" | custom-call | tf_op jit(solution)/shard_map/pallas_call | solution.py:706
  95.1 1.5 %copy.16 = f32[1,256,64]{1,2,0:T(8,128)} copy(f32[1,256,64]{1,2,0:T(8,128)} %bitcast.23) | data formatting | bytes 131072
  (1 shorter events, 0.0 us)

commit v4 on v3

--- a/solution.py
+++ b/solution.py
@@ -15,7 +15,7 @@
 
 
 epsilon = 1e-06
-CUTS = 2
+CUTS = 1
 
 
 def entering(shard, axis, join, neutral):
@@ -546,8 +546,10 @@
             pass_on(h - 1)
         if h == 0:
             wo_pass(order[0])
-
-    for d in order[1:]:
+        if h == 1:
+            wo_pass(order[1])
+
+    for d in order[2:]:
         wo_pass(d)
     pass_on(heads - 1)
     for h in range(heads):

time: 97.9 us -> 89 us (0.909)
  Pallas kernels: 90.6 us -> 81.2 us
    pallas_call x1, Pallas kernels: 90.6 us -> 81.2 us  [fused_device(): pl.pallas_call(functools.partial(fused_kernel, sizes), out_shape=jax.Shap...]
where the time goes in v4:
time: 89 us; the launch traced here: 87.2 us
  Pallas kernels  81.2 us (91%)
  between operations  2.48 us (3%)
  other arithmetic  2.01 us (2%)
  local copies, waits for them, and re-layouts  1.47 us (2%)
    pallas_call x1, Pallas kernels, fused_device(): pl.pallas_call(functools.partial(fused_kernel, sizes), out_shape=jax.Shap...  81.2 us

profile of v4, /device:TPU:0, one launch (start us, length us, event | category | flops | bytes accessed | tf_op | source)
XLA Modules:
  0.0 87.2 jit_solution(17874579681244761580)
XLA Ops:
  0.7 1.4 %select_reduce_fusion = (f32[]{:T(128)}, f32[]{:T(128)}) fusion(f32[1000]{0:T(1024)} %param.16, s32[]{:T(128)S(6)} %add.15, s32[]{:T(128)} %bitcast.18), kind=kLoop, calls=%fused_computation | loop fusion | flops 5998 | bytes 4016 | tf_op jit(solution)/shard_map/reduce_sum | solution.py:692
  3.9 0.6 convert_convert_fusion.embedded_ref
  4.5 81.2 %shard_map.127 = f32[64,256]{1,0:T(8,128)} custom-call(f32[64,256]{1,0:T(8,128)} %bitcast.24, f32[64,256]{1,0:T(8,128)} %bitcast.25, f32[1,256]{1,0:T(1,128)} %convert_convert_fusion.embedded_ref, f32[1,1]{1,0:T(1,128)} %bitcast.6.dt_ref, bf16[64,3072]{1,0:T(8,128)(2,1)} %embed_ref.1, f32[1,3072]{1,0:T(1,128)} %bitcast.26, f32[1,128]{1,0:T(1,128)} %bitcast.27, ...), custom_call_target="tpu_custom_call" | custom-call | tf_op jit(solution)/shard_map/pallas_call | solution.py:708
  85.7 1.5 %copy.16 = f32[1,256,64]{1,2,0:T(8,128)} copy(f32[1,256,64]{1,2,0:T(8,128)} %bitcast.23) | data formatting | bytes 131072
  (1 shorter events, 0.0 us)
